TPU v7x, 32 devices: a whole 2x2x4 slice. The times are simulated.
32 devices in a mesh: groups: 2 (over y), wide: 4 (over x, core), tp: 4 (over z).
Axes of the slice: x: 2, y: 2, z: 4, core: 2. Of those that a mesh axis runs over, the one named last changes fastest.
Arguments:
- patches: bfloat16 [2048, 1280], P(('groups', 'wide')), parts along dimension 0, may hold values from -190 to 190
- patch_counts: int32 [64], P('groups'), parts along dimension 0, may hold values from 24 to 32, as said below
- placement: int32 [64, 2], P('groups'), parts along dimension 0, may hold values from 0 to 511, as said below
- positions: int32 [3, 4096], P(None, ('groups', 'wide')), parts along dimension 1, may hold values from 0 to 2047
- text_embeds: bfloat16 [4096, 8192], P(('groups', 'wide'), 'tp'), parts along dimension 0, may hold values from -180 to 180
- vit_gain: float32 [1280], replicated, may hold values from 0.1 to 1.9
- vit_qkv: bfloat16 [1280, 3, 1280], P(None, None, 'tp'), may hold values from -4 to 4
- vit_proj: bfloat16 [1280, 1280], P('tp'), may hold values from -0.15625 to 0.15625
- merger_gain: float32 [1280], replicated, may hold values from 0.1 to 1.9
- merger_up: bfloat16 [5120, 2560], P(None, 'tp'), may hold values from -0.078125 to 0.078125
- merger_down: bfloat16 [2560, 8192], P('tp'), may hold values from -0.15625 to 0.15625
- llm_gain: float32 [8192], replicated, may hold values from 0.1 to 1.9
- llm_query: bfloat16 [8192, 4096], P('wide', 'tp'), may hold values from -0.0625 to 0.0625
- llm_key: bfloat16 [8192, 1024], P('wide', 'tp'), may hold values from -0.0625 to 0.0625
- llm_value: bfloat16 [8192, 1024], P('wide', 'tp'), may hold values from -0.0625 to 0.0625
Outputs:
- query: bfloat16 [4096, 4096], P(('groups', 'wide'), 'tp'), parts along dimension 0
- key_cache: bfloat16 [4096, 1024], P(('groups', 'wide'), 'tp'), parts along dimension 0
- value_cache: bfloat16 [4096, 1024], P(('groups', 'wide'), 'tp'), parts along dimension 0
There are 2 independent parts, one for each index of `groups`. A program takes and returns all parts, laid end to end along the dimension named above; an argument that names none is the same for every part. Nothing has to cross between parts.
Inputs may be any that keep to these rules, and one draw needn't show every extreme that they name: `patch_counts`: each count is a multiple of 4; images 8 * s to 8 * s + 7 belong to encoder device s of the wide axis; patch rows 4 m to 4 m + 3 of an image form its merged row m. `placement`: column 0 is the owner on the wide axis, column 1 the first of the image's merged rows among that owner's 512 rows. Images' merged rows never intersect and stay within the owner's rows. Each owner receives 8 images. At most 16 merged rows go from one encoder device to one owner, and that number is reached in every draw.
All inputs are finite; a program needn't handle non-finite values.
Results may differ from a plain program's by a relative error of at most 0.015.
Values may be sent and summed in bfloat16 or wider, within the bound.
No kernel may reach another device: no remote copies, remote signals or barrier semaphores. Data moves between devices by JAX's collectives and lax.ppermute only.
A program may use at most 128 MiB of HBM per device.

v0:
```python
import jax
import jax.numpy as jnp
from jax import lax
from jax.sharding import PartitionSpec as P

VD = 1280
HD = 128
IMG_DEV = 8
MAXP = 32
TOK_DEV = 512
VHD = 80
MAXM = 8
NORM_EPS = 1e-06
ROPE_BASE = 1000000.0


def layer_norm(inputs, scale_gain):
    center = jnp.mean(inputs, axis=-1, keepdims=True)
    shifted = inputs - center
    spread = jnp.mean(shifted * shifted, axis=-1, keepdims=True)
    return shifted * lax.rsqrt(spread + NORM_EPS) * scale_gain


def rms_norm(inputs, scale_gain):
    square = jnp.mean(inputs * inputs, axis=-1, keepdims=True)
    return inputs * lax.rsqrt(square + NORM_EPS) * scale_gain


def rotary(values, positions):
    half_size = HD // 2
    frequency = jnp.arange(half_size).astype(jnp.float32)
    inverse = ROPE_BASE ** (-2.0 * frequency / HD)
    first_end = HD // 8
    second = first_end + 3 * HD // 16
    ordinal = jnp.arange(half_size)
    section = jnp.where(ordinal < first_end, 0, jnp.where(ordinal < second, 1, 2))
    chosen = jnp.where(
        section[:, None] == 0,
        positions[0][None, :],
        jnp.where(section[:, None] == 1, positions[1][None, :], positions[2][None, :]),
    )
    angles = chosen.T.astype(jnp.float32) * inverse[None, :]
    angles = jnp.concatenate([angles, angles], axis=1)
    cosine = jnp.cos(angles)[:, None, :]
    sine_table = jnp.sin(angles)[:, None, :]
    upper_half = values[..., :half_size]
    lower_half = values[..., half_size:]
    turned = jnp.concatenate([-lower_half, upper_half], axis=-1)
    return values * cosine + turned * sine_table


def handoff_tables(patch_counts, placement, width_wide, myself, capacity):
    merged_count = patch_counts // 4
    owners = placement[:, 0]
    starts = placement[:, 1]
    owner_grid = owners.reshape(width_wide, IMG_DEV)
    count_grid = merged_count.reshape(width_wide, IMG_DEV)
    ordinal = jnp.arange(IMG_DEV)
    before = ordinal[:, None] < ordinal[None, :]
    same_owner = owner_grid[:, :, None] == owner_grid[:, None, :]
    offsets = jnp.sum(jnp.where(same_owner & before[None], count_grid[:, :, None], 0), axis=1)
    mine_owner = lax.dynamic_index_in_dim(owner_grid, myself, 0, keepdims=False)
    mine_count = lax.dynamic_index_in_dim(count_grid, myself, 0, keepdims=False)
    mine_offset = lax.dynamic_index_in_dim(offsets, myself, 0, keepdims=False)
    target = jnp.arange(width_wide)[:, None, None]
    slot_index = jnp.arange(capacity)[None, :, None]
    matches = (
        (mine_owner[None, None, :] == target)
        & (slot_index >= mine_offset[None, None, :])
        & (slot_index < mine_offset[None, None, :] + mine_count[None, None, :])
    )
    source_row = ordinal[None, None, :] * MAXM + slot_index - mine_offset[None, None, :]
    send_index = jnp.sum(jnp.where(matches, source_row, 0), axis=-1)
    send_live = jnp.any(matches, axis=-1)
    row_place = jnp.arange(TOK_DEV)[:, None]
    inside = (
        (owners[None, :] == myself)
        & (row_place >= starts[None, :])
        & (row_place < starts[None, :] + merged_count[None, :])
    )
    image_source = jnp.arange(owners.shape[0]) // IMG_DEV
    flat_slot = (
        image_source[None, :] * capacity
        + offsets.reshape(-1)[None, :]
        + row_place
        - starts[None, :]
    )
    take_index = jnp.sum(jnp.where(inside, flat_slot, 0), axis=-1)
    take_live = jnp.any(inside, axis=-1)
    return (send_index, send_live, take_index, take_live)


def pack_rows(visual, send_index, send_live):
    picked = jnp.take(visual, send_index.reshape(-1), axis=0)
    picked = picked.reshape(send_index.shape + (visual.shape[1],))
    return jnp.where(send_live[..., None], picked, jnp.zeros((), visual.dtype))


def place_rows(incoming, take_index, take_live, text_rows):
    flattened = incoming.reshape(-1, incoming.shape[-1])
    picked = jnp.take(flattened, take_index, axis=0)
    return jnp.where(take_live[:, None], picked, text_rows)


def per_device(
    patches,
    patch_counts,
    placement,
    positions,
    text_embeds,
    vit_gain,
    vit_qkv,
    vit_proj,
    merger_gain,
    merger_up,
    merger_down,
    llm_gain,
    llm_query,
    llm_key,
    llm_value,
):
    width_wide = lax.axis_size("wide")
    myself = lax.axis_index("wide")
    capacity = MAXM * ((IMG_DEV + width_wide - 1) // width_wide)
    local_heads = vit_qkv.shape[2] // VHD
    patch_rows = patches.astype(jnp.float32)
    normed = layer_norm(patch_rows, vit_gain).astype(jnp.bfloat16)
    triple = jnp.dot(normed, vit_qkv.reshape(VD, -1), preferred_element_type=jnp.float32).astype(
        jnp.bfloat16
    )
    triple = triple.reshape(IMG_DEV, MAXP, 3, local_heads, VHD)
    scores = jnp.einsum(
        "iqhd,ikhd->ihqk", triple[:, :, 0], triple[:, :, 1], preferred_element_type=jnp.float32
    ) * VHD ** (-0.5)
    own_counts = lax.dynamic_slice_in_dim(patch_counts, myself * IMG_DEV, IMG_DEV)
    present = jnp.arange(MAXP)[None, :] < own_counts[:, None]
    scores = jnp.where(present[:, None, None, :], scores, -jnp.inf)
    highest = jnp.max(scores, axis=-1, keepdims=True)
    raised = jnp.exp(scores - highest)
    attention_weights = (raised / jnp.sum(raised, axis=-1, keepdims=True)).astype(jnp.bfloat16)
    context = jnp.einsum(
        "ihqk,ikhd->iqhd", attention_weights, triple[:, :, 2], preferred_element_type=jnp.float32
    ).astype(jnp.bfloat16)
    context = context.reshape(IMG_DEV * MAXP, local_heads * VHD)
    partial_heads = jnp.dot(context, vit_proj, preferred_element_type=jnp.float32)
    attended = lax.psum(partial_heads.astype(jnp.bfloat16), "tp").astype(jnp.float32)
    mixed_rows = patch_rows + attended
    merged_in = (
        layer_norm(mixed_rows, merger_gain).astype(jnp.bfloat16).reshape(IMG_DEV * MAXM, 4 * VD)
    )
    hidden = jax.nn.gelu(
        jnp.dot(merged_in, merger_up, preferred_element_type=jnp.float32), approximate=False
    ).astype(jnp.bfloat16)
    partial_visual = jnp.dot(hidden, merger_down, preferred_element_type=jnp.float32)
    send_index, send_live, take_index, take_live = handoff_tables(
        patch_counts, placement, width_wide, myself, capacity
    )
    visual = lax.psum_scatter(
        partial_visual.astype(jnp.bfloat16), "tp", scatter_dimension=1, tiled=True
    )
    outgoing = pack_rows(visual, send_index, send_live)
    incoming = lax.all_to_all(outgoing, "wide", split_axis=0, concat_axis=0, tiled=True)
    prompt_slice = place_rows(incoming, take_index, take_live, text_embeds)
    prompt_rows = lax.all_gather(prompt_slice, "tp", axis=1, tiled=True)
    normed_prompt = rms_norm(prompt_rows.astype(jnp.float32), llm_gain).astype(jnp.bfloat16)
    weight_rows = (
        lax.all_gather(llm_query, "wide", axis=0, tiled=True),
        lax.all_gather(llm_key, "wide", axis=0, tiled=True),
        lax.all_gather(llm_value, "wide", axis=0, tiled=True),
    )
    projected_query, projected_key, projected_value = tuple(
        (
            jnp.dot(normed_prompt, matrix_rows, preferred_element_type=jnp.float32)
            for matrix_rows in weight_rows
        )
    )
    queries = (
        rotary(projected_query.reshape(TOK_DEV, -1, HD), positions)
        .astype(jnp.bfloat16)
        .reshape(TOK_DEV, -1)
    )
    key_rows = (
        rotary(projected_key.reshape(TOK_DEV, -1, HD), positions)
        .astype(jnp.bfloat16)
        .reshape(TOK_DEV, -1)
    )
    value_rows = projected_value.astype(jnp.bfloat16)
    return (queries, key_rows, value_rows)


def solution(mesh):
    return jax.shard_map(
        per_device,
        mesh=mesh,
        in_specs=(
            P(("groups", "wide"), None),
            P("groups"),
            P("groups", None),
            P(None, ("groups", "wide")),
            P(("groups", "wide"), "tp"),
            P(),
            P(None, None, "tp"),
            P("tp", None),
            P(),
            P(None, "tp"),
            P("tp", None),
            P(),
            P("wide", "tp"),
            P("wide", "tp"),
            P("wide", "tp"),
        ),
        out_specs=(
            P(("groups", "wide"), "tp"),
            P(("groups", "wide"), "tp"),
            P(("groups", "wide"), "tp"),
        ),
        check_vma=False,
    )
```

profile of v0, /device:TPU:0, one launch (start us, length us, event | category | flops | bytes accessed | tf_op | source)
XLA Modules:
  0.0 468.5 jit_solution(7635394783025104218)
XLA Ops:
  7.2 1.4 convert_reduce_fusion
  8.6 1.4 fusion.7
  10.1 2.0 convolution_convert_fusion.2
  15.2 1.3 convolution_convert_fusion.1
  17.1 42.7 %all-reduce.2.cloned.1.call-done = bf16[256,1280]{1,0:T(8,128)(2,1)} async-done(((bf16[256,1280]{1,0:T(8,128)(2,1)}), bf16[256,1280]{1,0:T(8,128)(2,1)}) %all-reduce.2.cloned.1.call-update) | async-done | bytes 655376 | tf_op jit(solution)/shard_map/psum | solution.py:146
  59.8 1.4 fusion.14
  61.2 1.4 multiply_reduce_fusion
  63.4 10.2 %convolution_convert_fusion = bf16[64,8192]{1,0:T(8,128)(2,1)} fusion(bf16[640,8192]{1,0:T(8,128)(2,1)} %param.25, bf16[64,5120]{1,0:T(8,128)(2,1)S(1)} %reshape.472, bf16[5120,640]{1,0:T(8,128)(2,1)} %param.24), kind=kOutput, calls=%fused_computation.8 | convolution fusion | flops 1093705728 | bytes 18743296 | tf_op jit(solution)/shard_map/dot_general | solution.py:154
  74.3 26.4 %reduce-scatter.2.cloned.1.call-done = bf16[64,2048]{1,0:T(8,128)(2,1)} async-done(((bf16[64,8192]{1,0:T(8,128)(2,1)}), bf16[64,2048]{1,0:T(8,128)(2,1)}) %reduce-scatter.2.cloned.1.call-update) | async-done | bytes 262160 | tf_op jit(solution)/shard_map/reduce_scatter | solution.py:158
  100.6 2.0 gather_fusion
  103.4 3.4 all-to-all-start
  106.9 5.9 %all-to-all-done = bf16[4,16,2048]{2,1,0:T(8,128)(2,1)S(1)} async-done(((bf16[4,16,2048]{2,1,0:T(8,128)(2,1)}), bf16[4,16,2048]{2,1,0:T(8,128)(2,1)S(1)}, u32[]{:S(2)}, u32[]{:S(2)}) %all-to-all-start) | async-done | bytes 262176 | tf_op jit(solution)/shard_map/all_to_all | solution.py:162
  112.8 2.5 gather_fusion.1
  115.3 3.3 select_select_fusion
  120.7 1.1 fusion.23
  122.1 143.8 %all-gather.5.cloned.1.call-done = bf16[512,8192]{1,0:T(8,128)(2,1)} async-done(((bf16[512,2048]{1,0:T(8,128)(2,1)}), bf16[512,8192]{1,0:T(8,128)(2,1)}) %all-gather.5.cloned.1.call-update) | async-done | bytes 8388624 | tf_op jit(solution)/shard_map/all_gather | solution.py:164
  265.9 5.1 %fusion.1 = f32[512]{0:T(512)S(1)} fusion(bf16[512,8192]{1,0:T(8,128)(2,1)} %all-gather.5.cloned.1.call-done), kind=kLoop, calls=%fused_computation.5 | loop fusion | flops 12582400 | bytes 8390656 | tf_op jit(solution)/shard_map/reduce_sum | solution.py:25
  271.0 29.0 %all-gather.9.cloned.1.call-done = bf16[8192,256]{1,0:T(8,128)(2,1)} async-done(((bf16[2048,256]{1,0:T(8,128)(2,1)}), bf16[8192,256]{1,0:T(8,128)(2,1)}) %all-gather.9.cloned.1.call-update) | async-done | bytes 4194320 | tf_op jit(solution)/shard_map/all_gather | solution.py:168
  300.0 7.6 %fusion.109 = f32[512,256]{0,1:T(8,128)S(1)} fusion(bf16[8192,256]{1,0:T(8,128)(2,1)} %all-gather.9.cloned.1.call-done, bf16[512,8192]{1,0:T(8,128)(2,1)} %all-gather.5.cloned.1.call-done, f32[8192]{0:T(1024)S(1)} %copy-done.9, f32[512]{0:T(512)S(1)} %add_rsqrt_fusion), kind=kOutput, calls=%fused_computation.191 | convolution fusion | flops 2164260864 | bytes 13142016 | tf_op jit(solution)/shard_map/dot_general | solution.py:173
  308.7 27.2 %all-gather.11.cloned.1.call-done = bf16[8192,256]{1,0:T(8,128)(2,1)} async-done(((bf16[2048,256]{1,0:T(8,128)(2,1)}), bf16[8192,256]{1,0:T(8,128)(2,1)}) %all-gather.11.cloned.1.call-update) | async-done | bytes 4194320 | tf_op jit(solution)/shard_map/all_gather | solution.py:169
  335.9 7.7 %convolution_convert_fusion.4 = bf16[512,256]{1,0:T(8,128)(2,1)} fusion(bf16[8192,256]{1,0:T(8,128)(2,1)} %all-gather.11.cloned.1.call-done, bf16[512,8192]{1,0:T(8,128)(2,1)} %all-gather.5.cloned.1.call-done, f32[8192]{0:T(1024)S(1)} %copy-done.9, f32[512]{0:T(512)S(1)} %add_rsqrt_fusion), kind=kOutput, calls=%fused_computation.34 | convolution fusion | flops 2164391936 | bytes 12879872 | tf_op jit(solution)/shard_map/dot_general | solution.py:173
  343.6 99.7 %all-gather.7.cloned.1.call-done = bf16[8192,1024]{1,0:T(8,128)(2,1)} async-done(((bf16[2048,1024]{1,0:T(8,128)(2,1)}), bf16[8192,1024]{1,0:T(8,128)(2,1)}) %all-gather.7.cloned.1.call-update) | async-done | bytes 16777232 | tf_op jit(solution)/shard_map/all_gather | solution.py:167
  443.2 14.7 %fusion.111 = f32[512,1024]{1,0:T(8,128)S(1)} fusion(bf16[8192,1024]{1,0:T(8,128)(2,1)} %all-gather.7.cloned.1.call-done, bf16[512,8192]{1,0:T(8,128)(2,1)} %all-gather.5.cloned.1.call-done, f32[8192]{0:T(1024)S(1)} %copy-done.9, f32[512]{0:T(512)S(1)} %add_rsqrt_fusion), kind=kOutput, calls=%fused_computation.192 | convolution fusion | flops 8606711808 | bytes 27297792 | tf_op jit(solution)/shard_map/dot_general | solution.py:173
  459.9 1.7 fusion.4
  (90 shorter events, 11.1 us)
Async XLA Ops:
  7.2 2.9 copy-start
  7.2 52.6 %all-reduce.2.cloned.1.call-start = ((), (), s32[]{:S(2)}) async-start(), calls=%async_computation.2 | async-start | bytes 1310720 | tf_op jit(solution)/shard_map/psum | solution.py:146
  12.1 1.4 copy-start.8
  14.0 1.1 copy-start.4
  14.6 2.0 copy-start.7
  14.7 45.2 %copy-start.2 = (bf16[256,1280]{1,0:T(8,128)(2,1)S(1)}, bf16[256,1280]{1,0:T(8,128)(2,1)}, u32[]{:S(2)}) copy-start(bf16[256,1280]{1,0:T(8,128)(2,1)} %param.15) | copy-start | bytes 1966084
  15.2 47.5 %copy-start.5 = (f32[1280]{0:T(1024)S(1)}, f32[1280]{0:T(1024)}, u32[]{:S(2)}) copy-start(f32[1280]{0:T(1024)} %param.23) | copy-start | bytes 15364
  16.5 84.1 %reduce-scatter.2.cloned.1.call-start = ((), (), s32[]{:S(2)}) async-start(), calls=%async_computation.3 | async-start | bytes 1310720 | tf_op jit(solution)/shard_map/reduce_scatter | solution.py:158
  59.8 2.9 copy-start.3
  103.4 9.4 %all-to-all-start = ((bf16[4,16,2048]{2,1,0:T(8,128)(2,1)}), bf16[4,16,2048]{2,1,0:T(8,128)(2,1)S(1)}, u32[]{:S(2)}, u32[]{:S(2)}) async-start(bf16[4,16,2048]{2,1,0:T(8,128)(2,1)} %select_select_fusion.1), calls=%async_computation.1 | async-start | bytes 524288 | tf_op jit(solution)/shard_map/all_to_all | solution.py:162
  106.8 159.1 %all-gather.5.cloned.1.call-start = ((), (), s32[]{:S(2)}) async-start(), calls=%async_computation.4 | async-start | bytes 10485760 | tf_op jit(solution)/shard_map/all_gather | solution.py:164
  118.6 181.4 %all-gather.9.cloned.1.call-start = ((), (), s32[]{:S(2)}) async-start(), calls=%async_computation.6 | async-start | bytes 5242880 | tf_op jit(solution)/shard_map/all_gather | solution.py:168
  119.2 216.8 %all-gather.11.cloned.1.call-start = ((), (), s32[]{:S(2)}) async-start(), calls=%async_computation.7 | async-start | bytes 5242880 | tf_op jit(solution)/shard_map/all_gather | solution.py:169
  119.7 0.7 copy-start.6
  119.8 323.5 %all-gather.7.cloned.1.call-start = ((), (), s32[]{:S(2)}) async-start(), calls=%async_computation.5 | async-start | bytes 20971520 | tf_op jit(solution)/shard_map/all_gather | solution.py:167
  122.1 177.9 %copy-start.9 = (f32[8192]{0:T(1024)S(1)}, f32[8192]{0:T(1024)}, u32[]{:S(2)}) copy-start(f32[8192]{0:T(1024)} %param.26) | copy-start | bytes 98308
  459.9 1.7 copy-start.1
Sparse Core Ops, SparseCore 0:
  16.7 43.0 all-reduce.1
  73.8 26.8 reduce-scatter.1
  118.7 147.1 all-gather.4
  267.3 32.6 all-gather.8
  301.4 34.4 all-gather.10
  337.3 105.8 all-gather.6
where the time goes:
time: 469 us; the launch traced here: 468 us
  waiting for transfers between devices  376 us (80%)
  matrix products  44.5 us (9%)
  other arithmetic  20.6 us (4%)
  between operations  14.5 us (3%)
  local copies, waits for them, and re-layouts  9 us (2%)
    all_gather x1, waiting for transfers between devices, per_device(): prompt_rows = lax.all_gather(prompt_slice, 'tp', axis=1, tiled=True)  144 us
    all_gather x1, waiting for transfers between devices, per_device(): lax.all_gather(llm_query, 'wide', axis=0, tiled=True)  99.7 us
    psum x1, waiting for transfers between devices, per_device(): lax.psum(partial_heads.astype(jnp.bfloat16), 'tp').astype(jnp.float32)  42.7 us
    dot_general x3, matrix products, per_device(): jnp.dot(normed_prompt, matrix_rows, preferred_element_type=jnp.float32)  30 us
    all_gather x1, waiting for transfers between devices, per_device(): lax.all_gather(llm_key, 'wide', axis=0, tiled=True)  29 us
    all_gather x1, waiting for transfers between devices, per_device(): lax.all_gather(llm_value, 'wide', axis=0, tiled=True)  27.2 us
    reduce_scatter x1, waiting for transfers between devices, per_device(): lax.psum_scatter(partial_visual.astype(jnp.bfloat16), 'tp', scatter_dimen...  26.4 us
    dot_general x1, matrix products, per_device(): jnp.dot(hidden, merger_down, preferred_element_type=jnp.float32)  10.2 us
  transfers between devices with their start and end apart: 7, of which 7 were waited for; matrix products, arithmetic and copies ran while one was open for 5% of the time, Pallas kernels for 0%

commit v1 on v0

--- a/solution.py
+++ b/solution.py
@@ -119,6 +119,15 @@
     llm_key,
     llm_value,
 ):
+
+    def solve_words_on_mesh(z):
+        slots = lax.axis_size("tp")
+        tray = [z]
+        for h in range(slots - 1):
+            tray.append(lax.ppermute(tray[-1], "tp", [(q, (q + 1) % slots) for q in range(slots)]))
+        res = jnp.roll(jnp.concatenate(tray[::-1], 1), (lax.axis_index("tp") + 1) * z.shape[1], 1)
+        return res
+
     width_wide = lax.axis_size("wide")
     myself = lax.axis_index("wide")
     capacity = MAXM * ((IMG_DEV + width_wide - 1) // width_wide)
@@ -161,7 +170,7 @@
     outgoing = pack_rows(visual, send_index, send_live)
     incoming = lax.all_to_all(outgoing, "wide", split_axis=0, concat_axis=0, tiled=True)
     prompt_slice = place_rows(incoming, take_index, take_live, text_embeds)
-    prompt_rows = lax.all_gather(prompt_slice, "tp", axis=1, tiled=True)
+    prompt_rows = solve_words_on_mesh(prompt_slice)
     normed_prompt = rms_norm(prompt_rows.astype(jnp.float32), llm_gain).astype(jnp.bfloat16)
     weight_rows = (
         lax.all_gather(llm_query, "wide", axis=0, tiled=True),

time: 469 us -> 324 us (0.69)
  waiting for transfers between devices: 376 us -> 217 us
  local copies, waits for them, and re-layouts: 9 us -> 25.7 us
    all_gather x1 -> x0, waiting for transfers between devices: 144 us -> none  [per_device(): prompt_rows = lax.all_gather(prompt_slice, 'tp', axis=1, tiled=True)]
    ppermute x0 -> x3, waiting for transfers between devices: none -> 142 us  [solve_words_on_mesh(): lax.ppermute(tray[-1], 'tp', [(q, (q + 1) % slots) for q in range(slots)])]
    all_gather x1, waiting for transfers between devices: 99.7 us -> 0.01 us  [per_device(): lax.all_gather(llm_query, 'wide', axis=0, tiled=True)]
    all_gather x1, waiting for transfers between devices: 29 us -> 0.02 us  [per_device(): lax.all_gather(llm_key, 'wide', axis=0, tiled=True)]
    all_gather x1, waiting for transfers between devices: 27.2 us -> 0.01 us  [per_device(): lax.all_gather(llm_value, 'wide', axis=0, tiled=True)]
    unnamed x22 -> x35, local copies, waits for them, and re-layouts: 1.65 us -> 16.5 us
  transfers between devices with their start and end apart: 7 -> 9, of which waited for: 7 -> 6; matrix products, arithmetic and copies ran while one was open for 5% -> 12% of each run, Pallas kernels for 0% -> 0%
where the time goes in v1:
time: 324 us
  waiting for transfers between devices  217 us (67%)
  matrix products  44.5 us (14%)
  local copies, waits for them, and re-layouts  25.7 us (8%)
  other arithmetic  16.6 us (5%)
  between operations  16.2 us (5%)
  starting transfers between devices  3.67 us (1%)
    ppermute x3, waiting for transfers between devices, solve_words_on_mesh(): lax.ppermute(tray[-1], 'tp', [(q, (q + 1) % slots) for q in range(slots)])  142 us
    psum x1, waiting for transfers between devices, per_device(): lax.psum(partial_heads.astype(jnp.bfloat16), 'tp').astype(jnp.float32)  43.2 us
    dot_general x3, matrix products, per_device(): jnp.dot(normed_prompt, matrix_rows, preferred_element_type=jnp.float32)  30 us
    reduce_scatter x1, waiting for transfers between devices, per_device(): lax.psum_scatter(partial_visual.astype(jnp.bfloat16), 'tp', scatter_dimen...  24 us
    unnamed x35, local copies, waits for them, and re-layouts  16.5 us
    dot_general x1, matrix products, per_device(): jnp.dot(hidden, merger_down, preferred_element_type=jnp.float32)  10.2 us
  transfers between devices with their start and end apart: 9, of which 6 were waited for; matrix products, arithmetic and copies ran while one was open for 12% of the time, Pallas kernels for 0%

profile of v1, /device:TPU:0, one launch (start us, length us, event | category | flops | bytes accessed | tf_op | source)
XLA Modules:
  0.0 323.5 jit_solution(11547811606439366905)
XLA Ops:
  11.7 2.0 convolution_convert_fusion.2
  18.0 43.2 %all-reduce.2.cloned.1.call-done = bf16[256,1280]{1,0:T(8,128)(2,1)} async-done(((bf16[256,1280]{1,0:T(8,128)(2,1)}), bf16[256,1280]{1,0:T(8,128)(2,1)}) %all-reduce.2.cloned.1.call-update) | async-done | bytes 655376 | tf_op jit(solution)/shard_map/psum | solution.py:155
  61.2 1.4 fusion.14
  62.6 1.4 multiply_reduce_fusion
  64.8 10.2 %convolution_convert_fusion = bf16[64,8192]{1,0:T(8,128)(2,1)} fusion(bf16[640,8192]{1,0:T(8,128)(2,1)} %param.25, bf16[64,5120]{1,0:T(8,128)(2,1)S(1)} %reshape.472, bf16[5120,640]{1,0:T(8,128)(2,1)} %param.24), kind=kOutput, calls=%fused_computation.8 | convolution fusion | flops 1093705728 | bytes 18743296 | tf_op jit(solution)/shard_map/dot_general | solution.py:163
  77.9 24.0 %reduce-scatter.2.cloned.1.call-done = bf16[64,2048]{1,0:T(8,128)(2,1)} async-done(((bf16[64,8192]{1,0:T(8,128)(2,1)}), bf16[64,2048]{1,0:T(8,128)(2,1)}) %reduce-scatter.2.cloned.1.call-update) | async-done | bytes 262160 | tf_op jit(solution)/shard_map/reduce_scatter | solution.py:167
  102.0 2.0 gather_fusion
  104.8 3.4 %all-to-all-start = ((bf16[4,16,2048]{2,1,0:T(8,128)(2,1)}), bf16[4,16,2048]{2,1,0:T(8,128)(2,1)S(1)}, u32[]{:S(2)}, u32[]{:S(2)}) async-start(bf16[4,16,2048]{2,1,0:T(8,128)(2,1)} %select_select_fusion.1), calls=%async_computation.1 | async-start | bytes 524288 | tf_op jit(solution)/shard_map/all_to_all | solution.py:171
  108.2 6.0 %all-to-all-done = bf16[4,16,2048]{2,1,0:T(8,128)(2,1)S(1)} async-done(((bf16[4,16,2048]{2,1,0:T(8,128)(2,1)}), bf16[4,16,2048]{2,1,0:T(8,128)(2,1)S(1)}, u32[]{:S(2)}, u32[]{:S(2)}) %all-to-all-start) | async-done | bytes 262176 | tf_op jit(solution)/shard_map/all_to_all | solution.py:171
  114.2 3.3 %gather_fusion.1 = bf16[512,2048]{1,0:T(8,128)(2,1)} fusion(bf16[64,2048]{1,0:T(8,128)(2,1)S(1)} %bitcast.76, s32[1024]{0:T(1024)S(1)} %pad_clamp_fusion), kind=kCustom, calls=%fused_computation.1 | custom fusion | bytes 4196352 | tf_op jit(solution)/shard_map/jit(_take)/gather | solution.py:101
  117.5 2.8 select_select_fusion
  120.4 48.7 %collective-permute-done = bf16[512,2048]{1,0:T(8,128)(2,1)S(1)} collective-permute-done((bf16[512,2048]{1,0:T(8,128)(2,1)S(1)}, bf16[512,2048]{1,0:T(8,128)(2,1)S(1)}, u32[]{:S(2)}, u32[]{:S(2)}) %collective-permute-start) | collective-permute-done | bytes 2097184 | tf_op jit(solution)/shard_map/ppermute | solution.py:127
  170.3 47.9 %collective-permute-done.1 = bf16[512,2048]{1,0:T(8,128)(2,1)} collective-permute-done((bf16[512,2048]{1,0:T(8,128)(2,1)S(1)}, bf16[512,2048]{1,0:T(8,128)(2,1)}, u32[]{:S(2)}, u32[]{:S(2)}) %collective-permute-start.1) | collective-permute-done | bytes 2097184 | tf_op jit(solution)/shard_map/ppermute | solution.py:127
  220.0 45.5 %collective-permute-done.2 = bf16[512,2048]{1,0:T(8,128)(2,1)} collective-permute-done((bf16[512,2048]{1,0:T(8,128)(2,1)}, bf16[512,2048]{1,0:T(8,128)(2,1)}, u32[]{:S(2)}, u32[]{:S(2)}) %collective-permute-start.2) | collective-permute-done | bytes 2097184 | tf_op jit(solution)/shard_map/ppermute | solution.py:127
  265.5 1.7 constant_dynamic-update-slice_fusion.7
  267.2 1.9 constant_dynamic-update-slice_fusion.6
  269.8 1.7 constant_dynamic-update-slice_fusion.3
  271.6 1.7 constant_dynamic-update-slice_fusion.2
  273.7 5.7 %copy-done.5 = bf16[512,16384]{1,0:T(8,128)(2,1)} copy-done((bf16[512,16384]{1,0:T(8,128)(2,1)}, bf16[512,16384]{1,0:T(8,128)(2,1)S(1)}, u32[]{:S(2)}) %copy-start.5) | copy-done | bytes 16777240
  279.4 1.7 fusion.1
  281.2 7.6 %fusion.109 = f32[512,256]{0,1:T(8,128)S(1)} fusion(bf16[8192,256]{1,0:T(8,128)(2,1)} %all-gather.6.cloned.1.call-done, f32[8192]{0:T(1024)S(1)} %copy-done.12, f32[512]{0:T(512)S(1)} %add_rsqrt_fusion, bf16[512,16384]{1,0:T(8,128)(2,1)} %copy-done.5, s32[]{:T(128)S(6)} %select_n.167), kind=kOutput, calls=%fused_computation.199 | convolution fusion | flops 2164260864 | bytes 13142020 | tf_op jit(solution)/shard_map/dot_general | solution.py:182
  289.9 7.7 %convolution_convert_fusion.4 = bf16[512,256]{1,0:T(8,128)(2,1)} fusion(bf16[8192,256]{1,0:T(8,128)(2,1)} %all-gather.8.cloned.1.call-done, f32[8192]{0:T(1024)S(1)} %copy-done.12, f32[512]{0:T(512)S(1)} %add_rsqrt_fusion, bf16[512,16384]{1,0:T(8,128)(2,1)} %copy-done.5, s32[]{:T(128)S(6)} %select_n.167), kind=kOutput, calls=%fused_computation.34 | convolution fusion | flops 2164391936 | bytes 12879876 | tf_op jit(solution)/shard_map/dot_general | solution.py:182
  297.6 14.7 %fusion.111 = f32[512,1024]{1,0:T(8,128)S(1)} fusion(bf16[8192,1024]{1,0:T(8,128)(2,1)} %all-gather.4.cloned.1.call-done, f32[8192]{0:T(1024)S(1)} %copy-done.12, f32[512]{0:T(512)S(1)} %add_rsqrt_fusion, bf16[512,16384]{1,0:T(8,128)(2,1)} %copy-done.5, s32[]{:T(128)S(6)} %select_n.167), kind=kOutput, calls=%fused_computation.200 | convolution fusion | flops 8606711808 | bytes 27297796 | tf_op jit(solution)/shard_map/dot_general | solution.py:182
  314.2 1.7 fusion.4
  (107 shorter events, 19.3 us)
Async XLA Ops:
  8.0 3.7 %copy-start = (bf16[1280,3,320]{0,2,1:T(8,128)(2,1)S(1)}, bf16[1280,3,320]{0,2,1:T(8,128)(2,1)}, u32[]{:S(2)}) copy-start(bf16[1280,3,320]{0,2,1:T(8,128)(2,1)} %param.21) | copy-start | bytes 7372804
  8.0 53.2 %all-reduce.2.cloned.1.call-start = ((), (), s32[]{:S(2)}) async-start(), calls=%async_computation.2 | async-start | bytes 1310720 | tf_op jit(solution)/shard_map/psum | solution.py:155
  15.4 1.1 copy-start.7
  15.8 45.4 %copy-start.2 = (bf16[256,1280]{1,0:T(8,128)(2,1)S(1)}, bf16[256,1280]{1,0:T(8,128)(2,1)}, u32[]{:S(2)}) copy-start(bf16[256,1280]{1,0:T(8,128)(2,1)} %param.15) | copy-start | bytes 1966084
  16.5 47.5 %copy-start.8 = (f32[1280]{0:T(1024)S(1)}, f32[1280]{0:T(1024)}, u32[]{:S(2)}) copy-start(f32[1280]{0:T(1024)} %param.23) | copy-start | bytes 15364
  17.9 84.1 %reduce-scatter.2.cloned.1.call-start = ((), (), s32[]{:S(2)}) async-start(), calls=%async_computation.3 | async-start | bytes 1310720 | tf_op jit(solution)/shard_map/reduce_scatter | solution.py:167
  61.2 2.9 copy-start.6
  75.0 206.1 %all-gather.6.cloned.1.call-start = ((), (), s32[]{:S(2)}) async-start(), calls=%async_computation.5 | async-start | bytes 5242880 | tf_op jit(solution)/shard_map/all_gather | solution.py:177
  75.6 1.2 copy-start.10
  75.6 1.2 copy-start.11
  75.6 214.3 %all-gather.8.cloned.1.call-start = ((), (), s32[]{:S(2)}) async-start(), calls=%async_computation.6 | async-start | bytes 5242880 | tf_op jit(solution)/shard_map/all_gather | solution.py:178
  76.2 221.3 %all-gather.4.cloned.1.call-start = ((), (), s32[]{:S(2)}) async-start(), calls=%async_computation.4 | async-start | bytes 20971520 | tf_op jit(solution)/shard_map/all_gather | solution.py:176
  104.8 9.4 %all-to-all-start = ((bf16[4,16,2048]{2,1,0:T(8,128)(2,1)}), bf16[4,16,2048]{2,1,0:T(8,128)(2,1)S(1)}, u32[]{:S(2)}, u32[]{:S(2)}) async-start(bf16[4,16,2048]{2,1,0:T(8,128)(2,1)} %select_select_fusion.1), calls=%async_computation.1 | async-start | bytes 524288 | tf_op jit(solution)/shard_map/all_to_all | solution.py:171
  117.5 100.8 %copy-start.9 = (s32[3,512]{1,0:T(4,128)S(1)}, s32[3,512]{1,0:T(4,128)}, u32[]{:S(2)}) copy-start(s32[3,512]{1,0:T(4,128)} %param.18) | copy-start | bytes 18436
  120.3 48.7 %collective-permute-start = (bf16[512,2048]{1,0:T(8,128)(2,1)S(1)}, bf16[512,2048]{1,0:T(8,128)(2,1)S(1)}, u32[]{:S(2)}, u32[]{:S(2)}) collective-permute-start(bf16[512,2048]{1,0:T(8,128)(2,1)S(1)} %select_select_fusion), channel_id=1, source_target_pairs={{0,1},{1,2},{2,3},{3,0},{4,5},{5,6},{6,7},{7,4},{8,9},{9,10},{10,1... | collective-permute-start | bytes 6291464 | tf_op jit(solution)/shard_map/ppermute | solution.py:127
  169.0 1.3 copy-start.3
  170.3 47.9 %collective-permute-start.1 = (bf16[512,2048]{1,0:T(8,128)(2,1)S(1)}, bf16[512,2048]{1,0:T(8,128)(2,1)}, u32[]{:S(2)}, u32[]{:S(2)}) collective-permute-start(bf16[512,2048]{1,0:T(8,128)(2,1)S(1)} %collective-permute-done), channel_id=1, source_target_pairs={{0,1},{1,2},{2,3},{3,0},{4,5},{5,6},{6,7},{7,4},{8,9},{9,10},{10,1... | collective-permute-start | bytes 6291464 | tf_op jit(solution)/shard_map/ppermute | solution.py:127
  218.2 47.3 %collective-permute-start.2 = (bf16[512,2048]{1,0:T(8,128)(2,1)}, bf16[512,2048]{1,0:T(8,128)(2,1)}, u32[]{:S(2)}, u32[]{:S(2)}) collective-permute-start(bf16[512,2048]{1,0:T(8,128)(2,1)} %collective-permute-done.1), channel_id=1, source_target_pairs={{0,1},{1,2},{2,3},{3,0},{4,5},{5,6},{6,7},{7,4},{8,9},{9,10},{10,1... | collective-permute-start | bytes 6291464 | tf_op jit(solution)/shard_map/ppermute | solution.py:127
  267.2 2.2 copy-start.4
  273.7 5.7 %copy-start.5 = (bf16[512,16384]{1,0:T(8,128)(2,1)}, bf16[512,16384]{1,0:T(8,128)(2,1)S(1)}, u32[]{:S(2)}) copy-start(bf16[512,16384]{1,0:T(8,128)(2,1)S(1)} %constant_dynamic-update-slice_fusion) | copy-start | bytes 50331652
  279.4 1.8 copy-start.12
  314.2 1.7 copy-start.1
Sparse Core Ops, SparseCore 0:
  18.0 43.0 all-reduce.1
  75.1 26.7 reduce-scatter.1
Sparse Core Ops, SparseCore 1:
  77.1 33.8 all-gather.5
  112.4 35.1 all-gather.7
  149.0 105.7 all-gather.3
